TPU v7x, 32 devices: a whole 2x2x4 slice. The times are simulated.
32 devices in a mesh: passage: 4 (over z), cell: 4 (over y, x), tm: 2 (over core).
Axes of the slice: x: 2, y: 2, z: 4, core: 2. Of those that a mesh axis runs over, the one named last changes fastest.
Arguments:
- adjoint_start: float32 [8, 5, 8, 1024, 256], P('tm', None, 'cell', 'passage'), may hold values from -6 to 6
- adjoint_source: float32 [8, 5, 8, 1024, 256], P('tm', None, 'cell', 'passage'), may hold values from -6 to 6
- jacobian: bfloat16 [2, 5, 5, 8, 1024, 256], P(None, None, None, 'cell', 'passage'), may hold values from -2.5 to 2.5
- pseudo_time: float32 [8, 1024, 256], P('cell', 'passage'), may hold values from 3 to 12
- dissipation: float32 [8, 1024, 256], P('cell', 'passage'), may hold values from 0.2 to 1
- surface_cells: int32 [4, 1024], P('cell'), may hold values from 0 to 1023, as said below
- surface_weights: float32 [8, 5, 4096], P('tm', None, 'cell'), may hold values from -1 to 1
Outputs:
- adjoint_final: float32 [8, 5, 8, 1024, 256], P('tm', None, 'cell', 'passage')
- diameter_modes: float32 [2, 16, 4096], P(None, None, 'cell')
Inputs may be any that keep to these rules, and one draw needn't show every extreme that they name: `surface_cells`: each row holds every value from 0 to 1023 exactly once, in a drawn order.
All inputs are finite; a program needn't handle non-finite values.
Results may differ from a plain program's by a relative error of at most 0.0025.
Values may be sent and summed in bfloat16 or wider, within the bound.
A program may use at most 256 MiB of HBM per device.

v0:
```python
import jax
import jax.numpy as jnp
from jax import lax
from jax.sharding import PartitionSpec as P

PASSAGES = 16
CJ = 64
SWEEPS = 2
OMEGA = 1.0


def with_halo(array, sides, width, wrap):
    for axis, dim in sides:
        peers, length = (lax.axis_size(axis), array.shape[dim])
        up = [(i, (i + 1) % peers) for i in range(peers if wrap else peers - 1)]
        down = [(j, i) for i, j in up]
        last = lax.slice_in_dim(array, length - width, length, axis=dim)
        leading = lax.slice_in_dim(array, 0, width, axis=dim)
        before = lax.ppermute(last, axis, up)
        after = lax.ppermute(leading, axis, down)
        array = jnp.concatenate([before, array, after], axis=dim)
    return array


def spectral_matrix(total):
    index = jnp.arange(total, dtype=jnp.int32)
    offset = index[:, None] - index[None, :]
    parity = (1 - 2 * (offset % 2)).astype(jnp.float32)
    phase_arg = jnp.pi * offset.astype(jnp.float32) / total
    sine_safe = jnp.where(offset == 0, jnp.float32(1.0), jnp.sin(phase_arg))
    values = 0.5 * parity * jnp.cos(phase_arg) / sine_safe
    return jnp.where(offset == 0, jnp.float32(0.0), values)


def blade_table(passages):
    index = jnp.arange(passages, dtype=jnp.int32)
    product_mod = index[:, None] * index[None, :] % passages
    phase_arg = 2.0 * jnp.pi * product_mod.astype(jnp.float32) / passages
    factor = 1.0 / passages**0.5
    return jnp.stack([jnp.cos(phase_arg), -jnp.sin(phase_arg)]) * factor


def adjoint_operator(field, plus_i, minus_i, plus_j, minus_j, jacobian, sigma, damping):
    total_out = sigma * field + damping * (4.0 * field - plus_i - minus_i - plus_j - minus_j)
    variables = field.shape[1]
    flux_rows = []
    for target_var in range(variables):
        acc_flux = jnp.zeros_like(field[:, 0])
        for source_var in range(variables):
            acc_flux = acc_flux + jacobian[0, source_var, target_var].astype(jnp.float32) * (
                field[:, source_var] - plus_i[:, source_var]
            )
            acc_flux = acc_flux + jacobian[1, source_var, target_var].astype(jnp.float32) * (
                field[:, source_var] - plus_j[:, source_var]
            )
        flux_rows.append(acc_flux)
    return total_out + jnp.stack(flux_rows, axis=1)


def neighbours(field):
    wrapped_field = with_halo(field, (("passage", 3),), 1, True)
    plus_j = wrapped_field[:, :, :, 2:]
    minus_j = wrapped_field[:, :, :, :-2]
    opened_field = with_halo(field.astype(jnp.bfloat16), (("cell", 2),), 1, False).astype(
        field.dtype
    )
    plus_i = opened_field[:, :, 2:]
    minus_i = opened_field[:, :, :-2]
    return (plus_i, minus_i, plus_j, minus_j)


def body(
    adjoint_start,
    adjoint_source,
    jacobian,
    pseudo_time,
    dissipation,
    surface_cells,
    surface_weights,
):
    local_times = adjoint_start.shape[0]
    all_times = local_times * lax.axis_size("tm")
    dmatrix = spectral_matrix(all_times)
    first_time = lax.axis_index("tm") * local_times
    start_rounded = adjoint_start.astype(jnp.bfloat16)
    own_columns = lax.dynamic_slice_in_dim(dmatrix, first_time, local_times, 1)
    spectral_term = OMEGA * jnp.einsum(
        "ab,avipk->bvipk",
        own_columns,
        lax.all_gather(start_rounded, "tm", axis=0, tiled=True).astype(jnp.float32),
        precision=lax.Precision.HIGHEST,
    )
    scaling = 1.0 / (pseudo_time + 4.0 * dissipation)
    field = adjoint_start
    for sweep_index in range(SWEEPS):
        plus_i, minus_i, plus_j, minus_j = neighbours(field)
        applied = adjoint_operator(
            field, plus_i, minus_i, plus_j, minus_j, jacobian, pseudo_time, dissipation
        )
        field = field + (adjoint_source - applied - spectral_term) * scaling
    variables = field.shape[1]
    stream_cells = field.shape[2]
    pitch_cells = field.shape[3]
    span_cells = field.shape[4]
    first_pitch = lax.axis_index("passage") * pitch_cells
    side_rows = (
        jnp.arange(PASSAGES, dtype=jnp.int32)[:, None] * CJ
        + jnp.arange(2, dtype=jnp.int32)[None, :] * (CJ - 1)
    ).reshape(2 * PASSAGES)
    local_rows = side_rows - first_pitch
    owned = (local_rows >= 0) & (local_rows < pitch_cells)
    clipped = jnp.clip(local_rows, 0, pitch_cells - 1)
    rows = jnp.take(field, clipped, axis=3)
    rows = jnp.where(owned[None, None, None, :, None], rows, jnp.float32(0.0))
    rows = rows.reshape(local_times, variables, stream_cells, PASSAGES, 2, span_cells)
    rows = rows.transpose(0, 1, 3, 4, 2, 5).reshape(
        local_times, variables, PASSAGES, 2 * stream_cells * span_cells
    )
    picked = jnp.take(rows, surface_cells[0], axis=3)
    partial_sens = jnp.einsum(
        "tvs,tvps->ps", surface_weights, picked, precision=lax.Precision.HIGHEST
    )
    table = blade_table(PASSAGES)
    mode_terms = jnp.einsum("cmp,ps->cms", table, partial_sens, precision=lax.Precision.HIGHEST)
    diameter_modes = lax.psum(mode_terms, ("passage", "tm"))
    return (field, diameter_modes)


def solution(mesh):
    in_specs = (
        P("tm", None, "cell", "passage", None),
        P("tm", None, "cell", "passage", None),
        P(None, None, None, "cell", "passage", None),
        P("cell", "passage", None),
        P("cell", "passage", None),
        P("cell", None),
        P("tm", None, "cell"),
    )
    out_specs = (P("tm", None, "cell", "passage", None), P(None, None, "cell"))
    return jax.shard_map(body, mesh=mesh, in_specs=in_specs, out_specs=out_specs, check_vma=False)
```

profile of v0, /device:TPU:0, one launch (start us, length us, event | category | flops | bytes accessed | tf_op | source)
XLA Modules:
  0.0 580.4 jit_solution(5656503605032928733)
XLA Ops:
  7.2 13.1 %copy.108 = bf16[4,5,2,256,256]{4,0,3,2,1:T(4,128)(2,1)} copy(f32[4,5,2,256,256]{4,3,2,1,0:T(8,128)} %param.7) | data formatting | bytes 15728640 | tf_op args[0]
  37.2 15.7 %constant_dynamic-update-slice_fusion.1 = (f32[4,5,2,257,256]{4,0,3,2,1:T(4,128)}, f32[4,5,2,256,256]{4,0,3,2,1:T(4,128)S(1)}) fusion(f32[4,5,2,256,256]{4,3,2,1,0:T(8,128)} %param.7), kind=kLoop, calls=%fused_computation.132 | loop fusion | bytes 31457280
  76.0 12.7 %collective-permute-done = bf16[4,5,1,256,256]{4,0,3,2,1:T(4,128)(2,1)S(1)} collective-permute-done((bf16[4,5,1,256,256]{4,0,3,2,1:T(4,128)(2,1)}, bf16[4,5,1,256,256]{4,0,3,2,1:T(4,128)(2,1)S(1)}, u32[]{:S(2)}, u32[]{:S(2)}) %collective-permute-start) | collective-permute-done | bytes 2621472 | tf_op jit(solution)/shard_map/ppermute | solution.py:19
  88.7 58.1 %collective-permute-done.1 = bf16[4,5,1,256,256]{4,0,3,2,1:T(4,128)(2,1)} collective-permute-done((bf16[4,5,1,256,256]{4,0,3,2,1:T(4,128)(2,1)}, bf16[4,5,1,256,256]{4,0,3,2,1:T(4,128)(2,1)}, u32[]{:S(2)}, u32[]{:S(2)}) %collective-permute-start.1) | collective-permute-done | bytes 2621472 | tf_op jit(solution)/shard_map/ppermute | solution.py:20
  146.8 13.4 %add_dynamic-update-slice_fusion.9 = (f32[4,5,2,256,256]{4,0,3,2,1:T(4,128)}, f32[4,1,2,256,256]{4,0,3,2,1:T(4,128)S(1)}, f32[4,1,2,256,256]{4,0,3,2,1:T(4,128)S...) fusion(f32[2,256,256]{2,1,0:T(8,128)} %get-tuple-element.76, ...), kind=kLoop, calls=%fused_computation.74 | loop fusion | flops 30932992 | bytes 59768832
  160.3 11.0 %add_dynamic-update-slice_fusion.8 = f32[4,5,2,256,256]{4,0,3,2,1:T(4,128)} fusion(f32[4,5,2,256,256]{4,0,3,2,1:T(4,128)} %get-tuple-element.25, f32[4,1,2,256,256]{4,0,3,2,1:T(4,128)} %get-tuple-element.35, f32[4,1,2,256,256]{4,0,3,2,1:T(4,128)S(1)} %get-tuple-element.34, f32[4,1,2,256,256]{4,0,3,2,1:T(4,128)S(1)} %get-tuple-element.33, ...), kind=kLoop, calls=%fused_computation.73 | loop fusion | flops 9961472 | bytes 28311552
  171.3 9.5 %add_dynamic-update-slice_fusion.7 = f32[4,5,2,256,256]{4,0,3,2,1:T(4,128)} fusion(f32[4,5,2,256,256]{4,0,3,2,1:T(4,128)} %add_dynamic-update-slice_fusion.8, f32[4,1,2,256,256]{4,0,3,2,1:T(4,128)} %get-tuple-element.35, f32[4,1,2,256,256]{4,0,3,2,1:T(4,128)S(1)} %get-tuple-element.34, f32[4,1,2,256,256]{4,0,3,2,1:T(4,128)S(1)} %get-tuple-element.33, ...), kind=kLoop, calls=%fused_computation.72 | loop fusion | flops 9961472 | bytes 28311552
  180.8 8.1 %add_dynamic-update-slice_fusion.6 = f32[4,5,2,256,256]{4,0,3,2,1:T(4,128)} fusion(f32[4,5,2,256,256]{4,0,3,2,1:T(4,128)} %add_dynamic-update-slice_fusion.7, f32[4,1,2,256,256]{4,0,3,2,1:T(4,128)} %get-tuple-element.35, f32[4,1,2,256,256]{4,0,3,2,1:T(4,128)} %copy-done.6, f32[4,1,2,256,256]{4,0,3,2,1:T(4,128)} %copy-done.5, ...), kind=kLoop, calls=%fused_computation.71 | loop fusion | flops 9961472 | bytes 28311552
  188.9 8.0 %add_dynamic-update-slice_fusion.5 = f32[4,5,2,256,256]{4,0,3,2,1:T(4,128)} fusion(f32[4,5,2,256,256]{4,0,3,2,1:T(4,128)} %add_dynamic-update-slice_fusion.6, f32[4,1,2,256,256]{4,0,3,2,1:T(4,128)} %get-tuple-element.35, f32[4,1,2,256,256]{4,0,3,2,1:T(4,128)} %copy-done.6, f32[4,1,2,256,256]{4,0,3,2,1:T(4,128)} %copy-done.5, ...), kind=kLoop, calls=%fused_computation.70 | loop fusion | flops 9961472 | bytes 28311552 | tf_op jit(solution)/shard_map/stack | solution.py:57
  197.0 13.2 %maximum_convert_fusion = f32[4,5,4,256,256]{4,0,3,2,1:T(4,128)} fusion(bf16[4,5,1,256,256]{4,0,3,2,1:T(4,128)(2,1)} %collective-permute-done.1, bf16[4,5,2,256,256]{4,0,3,2,1:T(4,128)(2,1)S(1)} %bitcast.179, bf16[4,5,1,256,256]{4,0,3,2,1:T(4,128)(2,1)} %copy-done.8), kind=kLoop, calls=%fused_computation.30 | loop fusion | flops 15728640 | bytes 31457280 | tf_op jit(solution)/shard_map/convert_element_type | solution.py:64
  210.2 44.5 %fusion.66 = (bf16[4,5,2,256,256]{4,0,3,2,1:T(4,128)(2,1)}, f32[4,5,2,256,256]{4,0,3,2,1:T(4,128)}, f32[4,5,2,256,256]{4,0,3,2,1:T(4,128)}) fusion(f32[4,5,2,256,256]{4,0,3,2,1:T(4,128)} %copy-done.7, f32[2,256,256]{2,1,0:T(8,128)S(1)} %copy-done.20, f32[4,5,2,256,256]{4,0,3,2,1:T(4,128)} %add_dynamic-update-slice_fusion.5, ...), kind=kOutput, calls=%fused_computation.184 | convolution fusion | flops 290979840 | bytes 101230592 | tf_op jit(solution)/shard_map/ab,avipk->bvipk/dot_general | solution.py:87
  278.4 42.3 %collective-permute-done.4 = bf16[4,5,1,256,256]{4,0,3,2,1:T(4,128)(2,1)S(1)} collective-permute-done((bf16[4,5,1,256,256]{4,0,3,2,1:T(4,128)(2,1)}, bf16[4,5,1,256,256]{4,0,3,2,1:T(4,128)(2,1)S(1)}, u32[]{:S(2)}, u32[]{:S(2)}) %collective-permute-start.4) | collective-permute-done | bytes 2621472 | tf_op jit(solution)/shard_map/ppermute | solution.py:19
  322.3 55.4 %collective-permute-done.5 = bf16[4,5,1,256,256]{4,0,3,2,1:T(4,128)(2,1)} collective-permute-done((bf16[4,5,1,256,256]{4,0,3,2,1:T(4,128)(2,1)}, bf16[4,5,1,256,256]{4,0,3,2,1:T(4,128)(2,1)}, u32[]{:S(2)}, u32[]{:S(2)}) %collective-permute-start.5) | collective-permute-done | bytes 2621472 | tf_op jit(solution)/shard_map/ppermute | solution.py:20
  377.7 18.1 %add_dynamic-update-slice_fusion.4 = (f32[4,5,2,256,256]{4,0,3,2,1:T(4,128)}, f32[4,1,2,256,256]{4,0,3,2,1:T(4,128)S(1)}, f32[4,1,2,256,256]{4,0,3,2,1:T(4,128)S...) fusion(f32[2,256,256]{2,1,0:T(8,128)} %get-tuple-element.76, ...), kind=kLoop, calls=%fused_computation.69 | loop fusion | flops 33554432 | bytes 59809792
  395.8 8.4 %add_dynamic-update-slice_fusion.3 = f32[4,5,2,256,256]{4,0,3,2,1:T(4,128)} fusion(f32[4,5,2,256,256]{4,0,3,2,1:T(4,128)} %get-tuple-element.12, f32[4,1,2,256,256]{4,0,3,2,1:T(4,128)S(1)} %get-tuple-element.22, f32[4,1,2,256,256]{4,0,3,2,1:T(4,128)S(1)} %get-tuple-element.21, f32[4,1,2,256,256]{4,0,3,2,1:T(4,128)S(1)} %get-tuple-element.20, ...), kind=kLoop, calls=%fused_computation.68 | loop fusion | flops 9961472 | bytes 28311552
  411.3 7.1 %add_dynamic-update-slice_fusion.1 = f32[4,5,2,256,256]{4,0,3,2,1:T(4,128)} fusion(f32[4,5,2,256,256]{4,0,3,2,1:T(4,128)} %add_dynamic-update-slice_fusion.2, f32[4,1,2,256,256]{4,0,3,2,1:T(4,128)S(1)} %get-tuple-element.22, f32[4,1,2,256,256]{4,0,3,2,1:T(4,128)S(1)} %get-tuple-element.21, f32[4,1,2,256,256]{4,0,3,2,1:T(4,128)S(1)} %get-tuple-element.20, ...), kind=kLoop, calls=%fused_computation.66 | loop fusion | flops 9961472 | bytes 28311552
  418.4 9.7 %add_dynamic-update-slice_fusion = f32[4,5,2,256,256]{4,0,3,2,1:T(4,128)} fusion(f32[4,5,2,256,256]{4,0,3,2,1:T(4,128)} %add_dynamic-update-slice_fusion.1, f32[4,1,2,256,256]{4,0,3,2,1:T(4,128)} %copy-done.4, f32[4,1,2,256,256]{4,0,3,2,1:T(4,128)} %copy-done.3, f32[4,1,2,256,256]{4,0,3,2,1:T(4,128)} %copy-done.2, f32[4,1,2,256,256]{4,0,3,2,1:T(4,128)} %copy-done.1, ...), kind=kLoop, calls=%fused_computation.65 | loop fusion | flops 9961472 | bytes 28311552 | tf_op jit(solution)/shard_map/stack | solution.py:57
  428.2 15.2 %maximum_convert_fusion.1 = f32[4,5,4,256,256]{4,0,3,2,1:T(4,128)} fusion(bf16[4,5,1,256,256]{4,0,3,2,1:T(4,128)(2,1)} %collective-permute-done.5, bf16[4,5,2,256,256]{4,0,3,2,1:T(4,128)(2,1)} %get-tuple-element.23, bf16[4,5,1,256,256]{4,0,3,2,1:T(4,128)(2,1)} %copy-done.9), kind=kLoop, calls=%fused_computation.31 | loop fusion | flops 15728640 | bytes 31457280 | tf_op jit(solution)/shard_map/convert_element_type | solution.py:64
  443.4 28.2 %multiply_add_fusion = f32[4,5,2,256,256]{4,0,3,2,1:T(4,128)} fusion(f32[4,5,2,256,256]{4,0,3,2,1:T(4,128)S(1)} %bitcast.181, f32[4,5,2,256,256]{4,0,3,2,1:T(4,128)} %get-tuple-element.97, f32[4,5,2,256,256]{4,0,3,2,1:T(4,128)} %add_dynamic-update-slice_fusion, f32[4,5,2,1,256]{4,0,3,2,1:T(4,128)} %collective-permute-done.7, ...), kind=kLoop, calls=%fused_computation.35 | loop fusion | flops 39321600 | bytes 75055104 | tf_op jit(solution)/shard_map/add | solution.py:100
  478.3 7.1 %copy.94 = f32[4,5,16,2,2,256]{2,0,5,4,3,1:T(4,128)} copy(f32[4,5,16,2,2,256]{5,4,3,2,1,0:T(2,128)S(1)} %fusion.28) | data formatting | bytes 2621440 | tf_op jit(solution)/shard_map/reshape | solution.py:116
  485.3 20.8 %gather_fusion.1 = f32[1024,4,5,16]{3,1,2,0:T(4,128)} fusion(f32[4,5,16,1024]{2,0,3,1:T(4,128)} %bitcast.182, s32[1024]{0:T(1024)S(1)} %copy-done.25), kind=kCustom, calls=%fused_computation.1 | custom fusion | bytes 2625536 | tf_op jit(solution)/shard_map/jit(_take)/gather | solution.py:119
  506.1 9.9 %multiply_reduce_fusion = f32[1024,16]{1,0:T(8,128)S(1)} fusion(f32[1024,4,5,16]{3,1,2,0:T(4,128)} %gather_fusion.1, f32[1024,4,5]{1,2,0:T(8,128)} %copy.96, pred[1024]{0:T(1024)(128)(4,1)S(1)} %copy-done.29), kind=kLoop, calls=%fused_computation.32 | loop fusion | flops 966656 | bytes 1459200
  517.3 10.1 %copy.85 = f32[4,5,2,256,256]{4,3,2,1,0:T(8,128)} copy(f32[4,5,2,256,256]{4,0,3,2,1:T(4,128)} %multiply_add_fusion) | data formatting | bytes 20971520
  527.4 44.4 %all-reduce.2.cloned.1.call-done = f32[2,16,1024]{2,1,0:T(8,128)} async-done(((f32[2,16,1024]{2,1,0:T(8,128)}), f32[2,16,1024]{2,1,0:T(8,128)}) %all-reduce.2.cloned.1.call-update) | async-done | bytes 131088 | tf_op jit(solution)/shard_map/psum | solution.py:125
  (128 shorter events, 81.6 us)
Async XLA Ops:
  7.2 203.1 %all-gather.2.cloned.1.call-start = ((), (), s32[]{:S(2)}) async-start(), calls=%async_computation | async-start | bytes 15728640 | tf_op jit(solution)/shard_map/all_gather | solution.py:90
  27.4 61.3 %collective-permute-start = (bf16[4,5,1,256,256]{4,0,3,2,1:T(4,128)(2,1)}, bf16[4,5,1,256,256]{4,0,3,2,1:T(4,128)(2,1)S(1)}, u32[]{:S(2)}, u32[]{:S(2)}) collective-permute-start(bf16[4,5,1,256,256]{4,0,3,2,1:T(4,128)(2,1)} %get-tuple-element.94), channel_id=1, source_target_pairs={{0,2},{2,4},{4,6},{1,3},{3,5},{5,7},{8,10},{10,12},{12,14},{9,11},... | collective-permute-start | bytes 7864328 | tf_op jit(solution)/shard_map/ppermute | solution.py:19
  32.4 114.4 %collective-permute-start.1 = (bf16[4,5,1,256,256]{4,0,3,2,1:T(4,128)(2,1)}, bf16[4,5,1,256,256]{4,0,3,2,1:T(4,128)(2,1)}, u32[]{:S(2)}, u32[]{:S(2)}) collective-permute-start(bf16[4,5,1,256,256]{4,0,3,2,1:T(4,128)(2,1)} %get-tuple-element.95), channel_id=1, source_target_pairs={{2,0},{4,2},{6,4},{3,1},{5,3},{7,5},{10,8},{12,10},{14,12},{11,9},... | collective-permute-start | bytes 7864328 | tf_op jit(solution)/shard_map/ppermute | solution.py:20
  37.0 25.3 %copy-start.14 = (f32[2,256,256]{2,1,0:T(8,128)S(1)}, f32[2,256,256]{2,1,0:T(8,128)}, u32[]{:S(2)}) copy-start(f32[2,256,256]{2,1,0:T(8,128)} %param.10) | copy-start | bytes 1572868
  37.0 534.8 %all-reduce.2.cloned.1.call-start = ((), (), s32[]{:S(2)}) async-start(), calls=%async_computation.1 | async-start | bytes 262144 | tf_op jit(solution)/shard_map/psum | solution.py:125
  37.2 25.1 %copy-start.17 = (f32[2,256,256]{2,1,0:T(8,128)S(1)}, f32[2,256,256]{2,1,0:T(8,128)}, u32[]{:S(2)}) copy-start(f32[2,256,256]{2,1,0:T(8,128)} %param.11) | copy-start | bytes 1572868
  37.2 30.3 %slice-start.5 = ((s8[13107200]{0:T(1024)(128)(4,1)}), s8[4194304]{0:T(1024)(128)(4,1)S(1)}, s32[]{:S(2)}) async-start(s8[13107200]{0:T(1024)(128)(4,1)} %bitcast.183), calls=%async_computation.7 | async-start | bytes 8388608
  37.2 30.3 %slice-start.6 = ((s8[13107200]{0:T(1024)(128)(4,1)}), s8[4194304]{0:T(1024)(128)(4,1)S(1)}, s32[]{:S(2)}) async-start(s8[13107200]{0:T(1024)(128)(4,1)} %bitcast.183), calls=%async_computation.8 | async-start | bytes 8388608
  37.2 30.3 %slice-start.7 = ((s8[13107200]{0:T(1024)(128)(4,1)}), s8[4194304]{0:T(1024)(128)(4,1)S(1)}, s32[]{:S(2)}) async-start(s8[13107200]{0:T(1024)(128)(4,1)} %bitcast.183), calls=%async_computation.9 | async-start | bytes 8388608
  58.6 16.7 %collective-permute-start.2 = (f32[4,5,2,1,256]{4,0,3,2,1:T(4,128)S(1)}, f32[4,5,2,1,256]{4,0,3,2,1:T(4,128)S(1)}, u32[]{:S(2)}, u32[]{:S(2)}) collective-permute-start(f32[4,5,2,1,256]{4,0,3,2,1:T(4,128)S(1)} %get-tuple-element.89), channel_id=1, source_target_pairs={{8,0},{16,8},{24,16},{0,24},{9,1},{17,9},{25,17},{1,25},{10,2},{18... | collective-permute-start | bytes 122888 | tf_op jit(solution)/shard_map/ppermute | solution.py:20
  62.3 147.9 %collective-permute-start.3 = (f32[4,5,2,1,256]{4,0,3,2,1:T(4,128)S(1)}, f32[4,5,2,1,256]{4,0,3,2,1:T(4,128)S(1)}, u32[]{:S(2)}, u32[]{:S(2)}) collective-permute-start(f32[4,5,2,1,256]{4,0,3,2,1:T(4,128)S(1)} %get-tuple-element.88), channel_id=1, source_target_pairs={{0,8},{8,16},{16,24},{24,0},{1,9},{9,17},{17,25},{25,1},{2,10},{10... | collective-permute-start | bytes 122888 | tf_op jit(solution)/shard_map/ppermute | solution.py:19
  67.5 121.4 %copy-start.10 = (f32[2,256,256]{2,1,0:T(8,128)}, f32[2,256,256]{2,1,0:T(8,128)S(1)}, u32[]{:S(2)}) copy-start(f32[2,256,256]{2,1,0:T(8,128)S(1)} %get-tuple-element.74) | copy-start | bytes 1572868
  88.7 58.1 %copy-start.8 = (bf16[4,5,1,256,256]{4,0,3,2,1:T(4,128)(2,1)}, bf16[4,5,1,256,256]{4,0,3,2,1:T(4,128)(2,1)S(1)}, u32[]{:S(2)}) copy-start(bf16[4,5,1,256,256]{4,0,3,2,1:T(4,128)(2,1)S(1)} %collective-permute-done) | copy-start | bytes 7864324
  180.8 16.1 %slice-start = ((s8[5242880]{0:T(1024)(128)(4,1)}), s8[4194304]{0:T(1024)(128)(4,1)S(1)}, s32[]{:S(2)}) async-start(s8[5242880]{0:T(1024)(128)(4,1)} %bitcast.178), calls=%async_computation.2 | async-start | bytes 8388608
  254.8 21.0 %copy-start.22 = (f32[4,5,1024]{2,0,1:T(4,128)S(1)}, f32[4,5,1024]{2,0,1:T(4,128)}, u32[]{:S(2)}) copy-start(f32[4,5,1024]{2,0,1:T(4,128)} %param.13) | copy-start | bytes 245764
  261.8 59.0 %collective-permute-start.4 = (bf16[4,5,1,256,256]{4,0,3,2,1:T(4,128)(2,1)}, bf16[4,5,1,256,256]{4,0,3,2,1:T(4,128)(2,1)S(1)}, u32[]{:S(2)}, u32[]{:S(2)}) collective-permute-start(bf16[4,5,1,256,256]{4,0,3,2,1:T(4,128)(2,1)} %get-tuple-element.92), channel_id=1, source_target_pairs={{0,2},{2,4},{4,6},{1,3},{3,5},{5,7},{8,10},{10,12},{12,14},{9,11},... | collective-permute-start | bytes 7864328 | tf_op jit(solution)/shard_map/ppermute | solution.py:19
  265.3 112.4 %collective-permute-start.5 = (bf16[4,5,1,256,256]{4,0,3,2,1:T(4,128)(2,1)}, bf16[4,5,1,256,256]{4,0,3,2,1:T(4,128)(2,1)}, u32[]{:S(2)}, u32[]{:S(2)}) collective-permute-start(bf16[4,5,1,256,256]{4,0,3,2,1:T(4,128)(2,1)} %get-tuple-element.93), channel_id=1, source_target_pairs={{2,0},{4,2},{6,4},{3,1},{5,3},{7,5},{10,8},{12,10},{14,12},{11,9},... | collective-permute-start | bytes 7864328 | tf_op jit(solution)/shard_map/ppermute | solution.py:20
  270.2 8.3 %collective-permute-start.6 = (f32[4,5,2,1,256]{4,0,3,2,1:T(4,128)S(1)}, f32[4,5,2,1,256]{4,0,3,2,1:T(4,128)S(1)}, u32[]{:S(2)}, u32[]{:S(2)}) collective-permute-start(f32[4,5,2,1,256]{4,0,3,2,1:T(4,128)S(1)} %get-tuple-element.87), channel_id=1, source_target_pairs={{8,0},{16,8},{24,16},{0,24},{9,1},{17,9},{25,17},{1,25},{10,2},{18... | collective-permute-start | bytes 122888 | tf_op jit(solution)/shard_map/ppermute | solution.py:20
  278.4 164.9 %collective-permute-start.7 = (f32[4,5,2,1,256]{4,0,3,2,1:T(4,128)}, f32[4,5,2,1,256]{4,0,3,2,1:T(4,128)}, u32[]{:S(2)}, u32[]{:S(2)}) collective-permute-start(f32[4,5,2,1,256]{4,0,3,2,1:T(4,128)} %get-tuple-element.86), channel_id=1, source_target_pairs={{0,8},{8,16},{16,24},{24,0},{1,9},{9,17},{17,25},{25,1},{2,10},{10... | collective-permute-start | bytes 122888 | tf_op jit(solution)/shard_map/ppermute | solution.py:19
  395.8 15.5 %copy-start.1 = (f32[4,1,2,256,256]{4,0,3,2,1:T(4,128)}, f32[4,1,2,256,256]{4,0,3,2,1:T(4,128)S(1)}, u32[]{:S(2)}) copy-start(f32[4,1,2,256,256]{4,0,3,2,1:T(4,128)S(1)} %get-tuple-element.19) | copy-start | bytes 6291460
  395.8 15.5 %copy-start.2 = (f32[4,1,2,256,256]{4,0,3,2,1:T(4,128)}, f32[4,1,2,256,256]{4,0,3,2,1:T(4,128)S(1)}, u32[]{:S(2)}) copy-start(f32[4,1,2,256,256]{4,0,3,2,1:T(4,128)S(1)} %get-tuple-element.20) | copy-start | bytes 6291460
  418.4 25.0 %slice-start.2 = ((s8[10485760]{0:T(1024)(128)(4,1)}), s8[4194304]{0:T(1024)(128)(4,1)S(1)}, s32[]{:S(2)}) async-start(s8[10485760]{0:T(1024)(128)(4,1)} %bitcast.180), calls=%async_computation.4 | async-start | bytes 8388608
  418.4 25.0 %slice-start.3 = ((s8[10485760]{0:T(1024)(128)(4,1)}), s8[4194304]{0:T(1024)(128)(4,1)S(1)}, s32[]{:S(2)}) async-start(s8[10485760]{0:T(1024)(128)(4,1)} %bitcast.180), calls=%async_computation.5 | async-start | bytes 8388608
  485.3 20.8 %copy-start.29 = (pred[1024]{0:T(1024)(128)(4,1)S(1)}, pred[1024]{0:T(1024)(128)(4,1)}, u32[]{:S(2)}) copy-start(pred[1024]{0:T(1024)(128)(4,1)} %compare_and_fusion) | copy-start | bytes 3076
  (25 other events, 272.4 us)
Sparse Core Ops, SparseCore 0:
  37.1 26.3 all-gather.1
  517.4 54.2 all-reduce.1
where the time goes:
time: 589 us; the launch traced here: 580 us
  waiting for transfers between devices  213 us (36%)
  other arithmetic  184 us (31%)
  local copies, waits for them, and re-layouts  105 us (18%)
  matrix products  45.8 us (8%)
  starting transfers between devices  18.7 us (3%)
  between operations  14.8 us (3%)
    ppermute x4, waiting for transfers between devices, with_halo(): after = lax.ppermute(leading, axis, down)  114 us
    unnamed x12, other arithmetic  92.5 us
    ppermute x4, waiting for transfers between devices, with_halo(): before = lax.ppermute(last, axis, up)  55 us
    unnamed x83, local copies, waits for them, and re-layouts  50.6 us
    dot_general x1, matrix products, body(): jnp.einsum('ab,avipk->bvipk', own_columns, lax.all_gather(start_rounded,...  44.5 us
    psum x1, waiting for transfers between devices, body(): diameter_modes = lax.psum(mode_terms, ('passage', 'tm'))  44.4 us
    convert_element_type x2, other arithmetic, neighbours(): with_halo(field.astype(jnp.bfloat16), (('cell', 2),), 1, False)  28.4 us
    add x1, other arithmetic, body(): field = field + (adjoint_source - applied - spectral_term) * scaling  28.2 us
  transfers between devices with their start and end apart: 10, of which 5 were waited for; matrix products, arithmetic and copies ran while one was open for 31% of the time, Pallas kernels for 0%

commit v1 on v0

--- a/solution.py
+++ b/solution.py
@@ -7,6 +7,10 @@
 CJ = 64
 SWEEPS = 2
 OMEGA = 1.0
+
+
+def view_edge_on_mesh(x_part):
+    return jnp.sum(lax.all_gather(x_part, ("passage", "tm")), 0)
 
 
 def with_halo(array, sides, width, wrap):
@@ -122,7 +126,7 @@
     )
     table = blade_table(PASSAGES)
     mode_terms = jnp.einsum("cmp,ps->cms", table, partial_sens, precision=lax.Precision.HIGHEST)
-    diameter_modes = lax.psum(mode_terms, ("passage", "tm"))
+    diameter_modes = view_edge_on_mesh(mode_terms)
     return (field, diameter_modes)
 
 

time: 589 us -> 557 us (0.946)
  waiting for transfers between devices: 213 us -> 180 us
    psum x1 -> x0, waiting for transfers between devices: 44.4 us -> none  [body(): diameter_modes = lax.psum(mode_terms, ('passage', 'tm'))]
    all_gather x0 -> x1, waiting for transfers between devices: none -> 11.6 us  [view_edge_on_mesh(): return jnp.sum(lax.all_gather(x_part, ('passage', 'tm')), 0)]
    unnamed x83 -> x82, local copies, waits for them, and re-layouts: 50.6 us -> 49 us
  transfers between devices with their start and end apart: 10 -> 10, of which waited for: 5 -> 5; matrix products, arithmetic and copies ran while one was open for 31% -> 33% of each run, Pallas kernels for 0% -> 0%
where the time goes in v1:
time: 557 us; the launch traced here: 548 us
  other arithmetic  185 us (33%)
  waiting for transfers between devices  180 us (32%)
  local copies, waits for them, and re-layouts  103 us (18%)
  matrix products  45.8 us (8%)
  starting transfers between devices  18.7 us (3%)
  between operations  14.8 us (3%)
    ppermute x4, waiting for transfers between devices, with_halo(): after = lax.ppermute(leading, axis, down)  114 us
    unnamed x12, other arithmetic  92.5 us
    ppermute x4, waiting for transfers between devices, with_halo(): before = lax.ppermute(last, axis, up)  55 us
    unnamed x82, local copies, waits for them, and re-layouts  49 us
    dot_general x1, matrix products, body(): jnp.einsum('ab,avipk->bvipk', own_columns, lax.all_gather(start_rounded,...  44.5 us
    convert_element_type x2, other arithmetic, neighbours(): with_halo(field.astype(jnp.bfloat16), (('cell', 2),), 1, False)  28.4 us
    add x1, other arithmetic, body(): field = field + (adjoint_source - applied - spectral_term) * scaling  28.2 us
    gather x1, local copies, waits for them, and re-layouts, body(): picked = jnp.take(rows, surface_cells[0], axis=3)  20.8 us
  transfers between devices with their start and end apart: 10, of which 5 were waited for; matrix products, arithmetic and copies ran while one was open for 33% of the time, Pallas kernels for 0%

profile of v1, /device:TPU:0, one launch (start us, length us, event | category | flops | bytes accessed | tf_op | source)
XLA Modules:
  0.0 548.0 jit_solution(1463579063515243113)
XLA Ops:
  7.2 13.1 %copy.108 = bf16[4,5,2,256,256]{4,0,3,2,1:T(4,128)(2,1)} copy(f32[4,5,2,256,256]{4,3,2,1,0:T(8,128)} %param.7) | data formatting | bytes 15728640 | tf_op args[0]
  37.2 15.7 %constant_dynamic-update-slice_fusion.1 = (f32[4,5,2,257,256]{4,0,3,2,1:T(4,128)}, f32[4,5,2,256,256]{4,0,3,2,1:T(4,128)S(1)}) fusion(f32[4,5,2,256,256]{4,3,2,1,0:T(8,128)} %param.7), kind=kLoop, calls=%fused_computation.132 | loop fusion | bytes 31457280
  76.0 12.7 %collective-permute-done = bf16[4,5,1,256,256]{4,0,3,2,1:T(4,128)(2,1)S(1)} collective-permute-done((bf16[4,5,1,256,256]{4,0,3,2,1:T(4,128)(2,1)}, bf16[4,5,1,256,256]{4,0,3,2,1:T(4,128)(2,1)S(1)}, u32[]{:S(2)}, u32[]{:S(2)}) %collective-permute-start) | collective-permute-done | bytes 2621472 | tf_op jit(solution)/shard_map/ppermute | solution.py:23
  88.7 58.1 %collective-permute-done.1 = bf16[4,5,1,256,256]{4,0,3,2,1:T(4,128)(2,1)} collective-permute-done((bf16[4,5,1,256,256]{4,0,3,2,1:T(4,128)(2,1)}, bf16[4,5,1,256,256]{4,0,3,2,1:T(4,128)(2,1)}, u32[]{:S(2)}, u32[]{:S(2)}) %collective-permute-start.1) | collective-permute-done | bytes 2621472 | tf_op jit(solution)/shard_map/ppermute | solution.py:24
  146.8 13.4 %add_dynamic-update-slice_fusion.9 = (f32[4,5,2,256,256]{4,0,3,2,1:T(4,128)}, f32[4,1,2,256,256]{4,0,3,2,1:T(4,128)S(1)}, f32[4,1,2,256,256]{4,0,3,2,1:T(4,128)S...) fusion(f32[2,256,256]{2,1,0:T(8,128)} %get-tuple-element.76, ...), kind=kLoop, calls=%fused_computation.74 | loop fusion | flops 30932992 | bytes 59768832
  160.3 11.0 %add_dynamic-update-slice_fusion.8 = f32[4,5,2,256,256]{4,0,3,2,1:T(4,128)} fusion(f32[4,5,2,256,256]{4,0,3,2,1:T(4,128)} %get-tuple-element.25, f32[4,1,2,256,256]{4,0,3,2,1:T(4,128)} %get-tuple-element.35, f32[4,1,2,256,256]{4,0,3,2,1:T(4,128)S(1)} %get-tuple-element.34, f32[4,1,2,256,256]{4,0,3,2,1:T(4,128)S(1)} %get-tuple-element.33, ...), kind=kLoop, calls=%fused_computation.73 | loop fusion | flops 9961472 | bytes 28311552
  171.3 9.5 %add_dynamic-update-slice_fusion.7 = f32[4,5,2,256,256]{4,0,3,2,1:T(4,128)} fusion(f32[4,5,2,256,256]{4,0,3,2,1:T(4,128)} %add_dynamic-update-slice_fusion.8, f32[4,1,2,256,256]{4,0,3,2,1:T(4,128)} %get-tuple-element.35, f32[4,1,2,256,256]{4,0,3,2,1:T(4,128)S(1)} %get-tuple-element.34, f32[4,1,2,256,256]{4,0,3,2,1:T(4,128)S(1)} %get-tuple-element.33, ...), kind=kLoop, calls=%fused_computation.72 | loop fusion | flops 9961472 | bytes 28311552
  180.8 8.1 %add_dynamic-update-slice_fusion.6 = f32[4,5,2,256,256]{4,0,3,2,1:T(4,128)} fusion(f32[4,5,2,256,256]{4,0,3,2,1:T(4,128)} %add_dynamic-update-slice_fusion.7, f32[4,1,2,256,256]{4,0,3,2,1:T(4,128)} %get-tuple-element.35, f32[4,1,2,256,256]{4,0,3,2,1:T(4,128)} %copy-done.6, f32[4,1,2,256,256]{4,0,3,2,1:T(4,128)} %copy-done.5, ...), kind=kLoop, calls=%fused_computation.71 | loop fusion | flops 9961472 | bytes 28311552
  188.9 8.0 %add_dynamic-update-slice_fusion.5 = f32[4,5,2,256,256]{4,0,3,2,1:T(4,128)} fusion(f32[4,5,2,256,256]{4,0,3,2,1:T(4,128)} %add_dynamic-update-slice_fusion.6, f32[4,1,2,256,256]{4,0,3,2,1:T(4,128)} %get-tuple-element.35, f32[4,1,2,256,256]{4,0,3,2,1:T(4,128)} %copy-done.6, f32[4,1,2,256,256]{4,0,3,2,1:T(4,128)} %copy-done.5, ...), kind=kLoop, calls=%fused_computation.70 | loop fusion | flops 9961472 | bytes 28311552 | tf_op jit(solution)/shard_map/stack | solution.py:61
  197.0 13.2 %maximum_convert_fusion = f32[4,5,4,256,256]{4,0,3,2,1:T(4,128)} fusion(bf16[4,5,1,256,256]{4,0,3,2,1:T(4,128)(2,1)} %collective-permute-done.1, bf16[4,5,2,256,256]{4,0,3,2,1:T(4,128)(2,1)S(1)} %bitcast.180, bf16[4,5,1,256,256]{4,0,3,2,1:T(4,128)(2,1)} %copy-done.8), kind=kLoop, calls=%fused_computation.30 | loop fusion | flops 15728640 | bytes 31457280 | tf_op jit(solution)/shard_map/convert_element_type | solution.py:68
  210.2 44.5 %fusion.66 = (bf16[4,5,2,256,256]{4,0,3,2,1:T(4,128)(2,1)}, f32[4,5,2,256,256]{4,0,3,2,1:T(4,128)}, f32[4,5,2,256,256]{4,0,3,2,1:T(4,128)}) fusion(f32[4,5,2,256,256]{4,0,3,2,1:T(4,128)} %copy-done.7, f32[2,256,256]{2,1,0:T(8,128)S(1)} %copy-done.20, f32[4,5,2,256,256]{4,0,3,2,1:T(4,128)} %add_dynamic-update-slice_fusion.5, ...), kind=kOutput, calls=%fused_computation.184 | convolution fusion | flops 290979840 | bytes 101230592 | tf_op jit(solution)/shard_map/ab,avipk->bvipk/dot_general | solution.py:91
  278.4 42.3 %collective-permute-done.4 = bf16[4,5,1,256,256]{4,0,3,2,1:T(4,128)(2,1)S(1)} collective-permute-done((bf16[4,5,1,256,256]{4,0,3,2,1:T(4,128)(2,1)}, bf16[4,5,1,256,256]{4,0,3,2,1:T(4,128)(2,1)S(1)}, u32[]{:S(2)}, u32[]{:S(2)}) %collective-permute-start.4) | collective-permute-done | bytes 2621472 | tf_op jit(solution)/shard_map/ppermute | solution.py:23
  322.3 55.4 %collective-permute-done.5 = bf16[4,5,1,256,256]{4,0,3,2,1:T(4,128)(2,1)} collective-permute-done((bf16[4,5,1,256,256]{4,0,3,2,1:T(4,128)(2,1)}, bf16[4,5,1,256,256]{4,0,3,2,1:T(4,128)(2,1)}, u32[]{:S(2)}, u32[]{:S(2)}) %collective-permute-start.5) | collective-permute-done | bytes 2621472 | tf_op jit(solution)/shard_map/ppermute | solution.py:24
  377.7 18.1 %add_dynamic-update-slice_fusion.4 = (f32[4,5,2,256,256]{4,0,3,2,1:T(4,128)}, f32[4,1,2,256,256]{4,0,3,2,1:T(4,128)S(1)}, f32[4,1,2,256,256]{4,0,3,2,1:T(4,128)S...) fusion(f32[2,256,256]{2,1,0:T(8,128)} %get-tuple-element.76, ...), kind=kLoop, calls=%fused_computation.69 | loop fusion | flops 33554432 | bytes 59809792
  395.8 8.4 %add_dynamic-update-slice_fusion.3 = f32[4,5,2,256,256]{4,0,3,2,1:T(4,128)} fusion(f32[4,5,2,256,256]{4,0,3,2,1:T(4,128)} %get-tuple-element.12, f32[4,1,2,256,256]{4,0,3,2,1:T(4,128)S(1)} %get-tuple-element.22, f32[4,1,2,256,256]{4,0,3,2,1:T(4,128)S(1)} %get-tuple-element.21, f32[4,1,2,256,256]{4,0,3,2,1:T(4,128)S(1)} %get-tuple-element.20, ...), kind=kLoop, calls=%fused_computation.68 | loop fusion | flops 9961472 | bytes 28311552
  411.3 7.1 %add_dynamic-update-slice_fusion.1 = f32[4,5,2,256,256]{4,0,3,2,1:T(4,128)} fusion(f32[4,5,2,256,256]{4,0,3,2,1:T(4,128)} %add_dynamic-update-slice_fusion.2, f32[4,1,2,256,256]{4,0,3,2,1:T(4,128)S(1)} %get-tuple-element.22, f32[4,1,2,256,256]{4,0,3,2,1:T(4,128)S(1)} %get-tuple-element.21, f32[4,1,2,256,256]{4,0,3,2,1:T(4,128)S(1)} %get-tuple-element.20, ...), kind=kLoop, calls=%fused_computation.66 | loop fusion | flops 9961472 | bytes 28311552
  418.4 9.7 %add_dynamic-update-slice_fusion = f32[4,5,2,256,256]{4,0,3,2,1:T(4,128)} fusion(f32[4,5,2,256,256]{4,0,3,2,1:T(4,128)} %add_dynamic-update-slice_fusion.1, f32[4,1,2,256,256]{4,0,3,2,1:T(4,128)} %copy-done.4, f32[4,1,2,256,256]{4,0,3,2,1:T(4,128)} %copy-done.3, f32[4,1,2,256,256]{4,0,3,2,1:T(4,128)} %copy-done.2, f32[4,1,2,256,256]{4,0,3,2,1:T(4,128)} %copy-done.1, ...), kind=kLoop, calls=%fused_computation.65 | loop fusion | flops 9961472 | bytes 28311552 | tf_op jit(solution)/shard_map/stack | solution.py:61
  428.2 15.2 %maximum_convert_fusion.1 = f32[4,5,4,256,256]{4,0,3,2,1:T(4,128)} fusion(bf16[4,5,1,256,256]{4,0,3,2,1:T(4,128)(2,1)} %collective-permute-done.5, bf16[4,5,2,256,256]{4,0,3,2,1:T(4,128)(2,1)} %get-tuple-element.23, bf16[4,5,1,256,256]{4,0,3,2,1:T(4,128)(2,1)} %copy-done.9), kind=kLoop, calls=%fused_computation.31 | loop fusion | flops 15728640 | bytes 31457280 | tf_op jit(solution)/shard_map/convert_element_type | solution.py:68
  443.4 28.2 %multiply_add_fusion = f32[4,5,2,256,256]{4,0,3,2,1:T(4,128)} fusion(f32[4,5,2,256,256]{4,0,3,2,1:T(4,128)S(1)} %bitcast.182, f32[4,5,2,256,256]{4,0,3,2,1:T(4,128)} %get-tuple-element.97, f32[4,5,2,256,256]{4,0,3,2,1:T(4,128)} %add_dynamic-update-slice_fusion, f32[4,5,2,1,256]{4,0,3,2,1:T(4,128)} %collective-permute-done.7, ...), kind=kLoop, calls=%fused_computation.35 | loop fusion | flops 39321600 | bytes 75055104 | tf_op jit(solution)/shard_map/add | solution.py:104
  478.3 7.1 %copy.94 = f32[4,5,16,2,2,256]{2,0,5,4,3,1:T(4,128)} copy(f32[4,5,16,2,2,256]{5,4,3,2,1,0:T(2,128)S(1)} %fusion.28) | data formatting | bytes 2621440 | tf_op jit(solution)/shard_map/reshape | solution.py:120
  485.3 20.8 %gather_fusion.1 = f32[1024,4,5,16]{3,1,2,0:T(4,128)} fusion(f32[4,5,16,1024]{2,0,3,1:T(4,128)} %bitcast.183, s32[1024]{0:T(1024)S(1)} %copy-done.25), kind=kCustom, calls=%fused_computation.1 | custom fusion | bytes 2625536 | tf_op jit(solution)/shard_map/jit(_take)/gather | solution.py:123
  506.1 9.9 %multiply_reduce_fusion = f32[1024,16]{1,0:T(8,128)S(1)} fusion(f32[1024,4,5,16]{3,1,2,0:T(4,128)} %gather_fusion.1, f32[1024,4,5]{1,2,0:T(8,128)} %copy.96, pred[1024]{0:T(1024)(128)(4,1)S(1)} %copy-done.29), kind=kLoop, calls=%fused_computation.32 | loop fusion | flops 966656 | bytes 1459200
  517.3 10.1 %copy.85 = f32[4,5,2,256,256]{4,3,2,1,0:T(8,128)} copy(f32[4,5,2,256,256]{4,0,3,2,1:T(4,128)} %multiply_add_fusion) | data formatting | bytes 20971520
  527.4 11.6 %all-gather.6.cloned.1.call-done = f32[16,16,1024]{2,1,0:T(8,128)} async-done(((f32[2,16,1024]{2,1,0:T(8,128)}), f32[16,16,1024]{2,1,0:T(8,128)}) %all-gather.6.cloned.1.call-update) | async-done | bytes 1048592 | tf_op jit(solution)/shard_map/all_gather | solution.py:13
  (128 shorter events, 81.9 us)
Async XLA Ops:
  7.2 203.1 %all-gather.4.cloned.1.call-start = ((), (), s32[]{:S(2)}) async-start(), calls=%async_computation | async-start | bytes 15728640 | tf_op jit(solution)/shard_map/all_gather | solution.py:94
  27.4 61.3 %collective-permute-start = (bf16[4,5,1,256,256]{4,0,3,2,1:T(4,128)(2,1)}, bf16[4,5,1,256,256]{4,0,3,2,1:T(4,128)(2,1)S(1)}, u32[]{:S(2)}, u32[]{:S(2)}) collective-permute-start(bf16[4,5,1,256,256]{4,0,3,2,1:T(4,128)(2,1)} %get-tuple-element.94), channel_id=1, source_target_pairs={{0,2},{2,4},{4,6},{1,3},{3,5},{5,7},{8,10},{10,12},{12,14},{9,11},... | collective-permute-start | bytes 7864328 | tf_op jit(solution)/shard_map/ppermute | solution.py:23
  32.4 114.4 %collective-permute-start.1 = (bf16[4,5,1,256,256]{4,0,3,2,1:T(4,128)(2,1)}, bf16[4,5,1,256,256]{4,0,3,2,1:T(4,128)(2,1)}, u32[]{:S(2)}, u32[]{:S(2)}) collective-permute-start(bf16[4,5,1,256,256]{4,0,3,2,1:T(4,128)(2,1)} %get-tuple-element.95), channel_id=1, source_target_pairs={{2,0},{4,2},{6,4},{3,1},{5,3},{7,5},{10,8},{12,10},{14,12},{11,9},... | collective-permute-start | bytes 7864328 | tf_op jit(solution)/shard_map/ppermute | solution.py:24
  37.0 25.3 %copy-start.14 = (f32[2,256,256]{2,1,0:T(8,128)S(1)}, f32[2,256,256]{2,1,0:T(8,128)}, u32[]{:S(2)}) copy-start(f32[2,256,256]{2,1,0:T(8,128)} %param.10) | copy-start | bytes 1572868
  37.0 502.1 %all-gather.6.cloned.1.call-start = ((), (), s32[]{:S(2)}) async-start(), calls=%async_computation.1 | async-start | bytes 1179648 | tf_op jit(solution)/shard_map/all_gather | solution.py:13
  37.2 25.1 %copy-start.17 = (f32[2,256,256]{2,1,0:T(8,128)S(1)}, f32[2,256,256]{2,1,0:T(8,128)}, u32[]{:S(2)}) copy-start(f32[2,256,256]{2,1,0:T(8,128)} %param.11) | copy-start | bytes 1572868
  37.2 30.3 %slice-start.5 = ((s8[13107200]{0:T(1024)(128)(4,1)}), s8[4194304]{0:T(1024)(128)(4,1)S(1)}, s32[]{:S(2)}) async-start(s8[13107200]{0:T(1024)(128)(4,1)} %bitcast.184), calls=%async_computation.7 | async-start | bytes 8388608
  37.2 30.3 %slice-start.6 = ((s8[13107200]{0:T(1024)(128)(4,1)}), s8[4194304]{0:T(1024)(128)(4,1)S(1)}, s32[]{:S(2)}) async-start(s8[13107200]{0:T(1024)(128)(4,1)} %bitcast.184), calls=%async_computation.8 | async-start | bytes 8388608
  37.2 30.3 %slice-start.7 = ((s8[13107200]{0:T(1024)(128)(4,1)}), s8[4194304]{0:T(1024)(128)(4,1)S(1)}, s32[]{:S(2)}) async-start(s8[13107200]{0:T(1024)(128)(4,1)} %bitcast.184), calls=%async_computation.9 | async-start | bytes 8388608
  58.6 16.7 %collective-permute-start.2 = (f32[4,5,2,1,256]{4,0,3,2,1:T(4,128)S(1)}, f32[4,5,2,1,256]{4,0,3,2,1:T(4,128)S(1)}, u32[]{:S(2)}, u32[]{:S(2)}) collective-permute-start(f32[4,5,2,1,256]{4,0,3,2,1:T(4,128)S(1)} %get-tuple-element.89), channel_id=1, source_target_pairs={{8,0},{16,8},{24,16},{0,24},{9,1},{17,9},{25,17},{1,25},{10,2},{18... | collective-permute-start | bytes 122888 | tf_op jit(solution)/shard_map/ppermute | solution.py:24
  62.3 147.9 %collective-permute-start.3 = (f32[4,5,2,1,256]{4,0,3,2,1:T(4,128)S(1)}, f32[4,5,2,1,256]{4,0,3,2,1:T(4,128)S(1)}, u32[]{:S(2)}, u32[]{:S(2)}) collective-permute-start(f32[4,5,2,1,256]{4,0,3,2,1:T(4,128)S(1)} %get-tuple-element.88), channel_id=1, source_target_pairs={{0,8},{8,16},{16,24},{24,0},{1,9},{9,17},{17,25},{25,1},{2,10},{10... | collective-permute-start | bytes 122888 | tf_op jit(solution)/shard_map/ppermute | solution.py:23
  67.5 121.4 %copy-start.10 = (f32[2,256,256]{2,1,0:T(8,128)}, f32[2,256,256]{2,1,0:T(8,128)S(1)}, u32[]{:S(2)}) copy-start(f32[2,256,256]{2,1,0:T(8,128)S(1)} %get-tuple-element.74) | copy-start | bytes 1572868
  88.7 58.1 %copy-start.8 = (bf16[4,5,1,256,256]{4,0,3,2,1:T(4,128)(2,1)}, bf16[4,5,1,256,256]{4,0,3,2,1:T(4,128)(2,1)S(1)}, u32[]{:S(2)}) copy-start(bf16[4,5,1,256,256]{4,0,3,2,1:T(4,128)(2,1)S(1)} %collective-permute-done) | copy-start | bytes 7864324
  180.8 16.1 %slice-start = ((s8[5242880]{0:T(1024)(128)(4,1)}), s8[4194304]{0:T(1024)(128)(4,1)S(1)}, s32[]{:S(2)}) async-start(s8[5242880]{0:T(1024)(128)(4,1)} %bitcast.179), calls=%async_computation.2 | async-start | bytes 8388608
  254.8 21.0 %copy-start.22 = (f32[4,5,1024]{2,0,1:T(4,128)S(1)}, f32[4,5,1024]{2,0,1:T(4,128)}, u32[]{:S(2)}) copy-start(f32[4,5,1024]{2,0,1:T(4,128)} %param.13) | copy-start | bytes 245764
  261.8 59.0 %collective-permute-start.4 = (bf16[4,5,1,256,256]{4,0,3,2,1:T(4,128)(2,1)}, bf16[4,5,1,256,256]{4,0,3,2,1:T(4,128)(2,1)S(1)}, u32[]{:S(2)}, u32[]{:S(2)}) collective-permute-start(bf16[4,5,1,256,256]{4,0,3,2,1:T(4,128)(2,1)} %get-tuple-element.92), channel_id=1, source_target_pairs={{0,2},{2,4},{4,6},{1,3},{3,5},{5,7},{8,10},{10,12},{12,14},{9,11},... | collective-permute-start | bytes 7864328 | tf_op jit(solution)/shard_map/ppermute | solution.py:23
  265.3 112.4 %collective-permute-start.5 = (bf16[4,5,1,256,256]{4,0,3,2,1:T(4,128)(2,1)}, bf16[4,5,1,256,256]{4,0,3,2,1:T(4,128)(2,1)}, u32[]{:S(2)}, u32[]{:S(2)}) collective-permute-start(bf16[4,5,1,256,256]{4,0,3,2,1:T(4,128)(2,1)} %get-tuple-element.93), channel_id=1, source_target_pairs={{2,0},{4,2},{6,4},{3,1},{5,3},{7,5},{10,8},{12,10},{14,12},{11,9},... | collective-permute-start | bytes 7864328 | tf_op jit(solution)/shard_map/ppermute | solution.py:24
  270.2 8.3 %collective-permute-start.6 = (f32[4,5,2,1,256]{4,0,3,2,1:T(4,128)S(1)}, f32[4,5,2,1,256]{4,0,3,2,1:T(4,128)S(1)}, u32[]{:S(2)}, u32[]{:S(2)}) collective-permute-start(f32[4,5,2,1,256]{4,0,3,2,1:T(4,128)S(1)} %get-tuple-element.87), channel_id=1, source_target_pairs={{8,0},{16,8},{24,16},{0,24},{9,1},{17,9},{25,17},{1,25},{10,2},{18... | collective-permute-start | bytes 122888 | tf_op jit(solution)/shard_map/ppermute | solution.py:24
  278.4 164.9 %collective-permute-start.7 = (f32[4,5,2,1,256]{4,0,3,2,1:T(4,128)}, f32[4,5,2,1,256]{4,0,3,2,1:T(4,128)}, u32[]{:S(2)}, u32[]{:S(2)}) collective-permute-start(f32[4,5,2,1,256]{4,0,3,2,1:T(4,128)} %get-tuple-element.86), channel_id=1, source_target_pairs={{0,8},{8,16},{16,24},{24,0},{1,9},{9,17},{17,25},{25,1},{2,10},{10... | collective-permute-start | bytes 122888 | tf_op jit(solution)/shard_map/ppermute | solution.py:23
  395.8 15.5 %copy-start.1 = (f32[4,1,2,256,256]{4,0,3,2,1:T(4,128)}, f32[4,1,2,256,256]{4,0,3,2,1:T(4,128)S(1)}, u32[]{:S(2)}) copy-start(f32[4,1,2,256,256]{4,0,3,2,1:T(4,128)S(1)} %get-tuple-element.19) | copy-start | bytes 6291460
  395.8 15.5 %copy-start.2 = (f32[4,1,2,256,256]{4,0,3,2,1:T(4,128)}, f32[4,1,2,256,256]{4,0,3,2,1:T(4,128)S(1)}, u32[]{:S(2)}) copy-start(f32[4,1,2,256,256]{4,0,3,2,1:T(4,128)S(1)} %get-tuple-element.20) | copy-start | bytes 6291460
  418.4 25.0 %slice-start.2 = ((s8[10485760]{0:T(1024)(128)(4,1)}), s8[4194304]{0:T(1024)(128)(4,1)S(1)}, s32[]{:S(2)}) async-start(s8[10485760]{0:T(1024)(128)(4,1)} %bitcast.181), calls=%async_computation.4 | async-start | bytes 8388608
  418.4 25.0 %slice-start.3 = ((s8[10485760]{0:T(1024)(128)(4,1)}), s8[4194304]{0:T(1024)(128)(4,1)S(1)}, s32[]{:S(2)}) async-start(s8[10485760]{0:T(1024)(128)(4,1)} %bitcast.181), calls=%async_computation.5 | async-start | bytes 8388608
  485.3 20.8 %copy-start.29 = (pred[1024]{0:T(1024)(128)(4,1)S(1)}, pred[1024]{0:T(1024)(128)(4,1)}, u32[]{:S(2)}) copy-start(pred[1024]{0:T(1024)(128)(4,1)} %compare_and_fusion) | copy-start | bytes 3076
  (25 other events, 272.4 us)
Sparse Core Ops, SparseCore 0:
  37.1 26.3 all-gather.3
  517.4 21.5 all-gather.5
